TPU v7x, 512 devices: a whole 4x4x16 slice. The times are simulated.
512 devices in a mesh: layer: 4 (over x), expert: 128 (over y, z, core).
Axes of the slice: x: 4, y: 4, z: 16, core: 2. Of those that a mesh axis runs over, the one named last changes fastest.
Arguments:
- grad_hidden: bfloat16 [131072, 384], P(('layer', 'expert')), parts along dimension 0, may hold values from -6 to 6
- grad_out: bfloat16 [131072, 1024], P(('layer', 'expert')), parts along dimension 0, may hold values from -0.41992188 to 0.41992188
- grad_route: int32 [131072, 1], P(('layer', 'expert')), parts along dimension 0, may hold values from 0 to 127; in each aligned block of 256 rows (0 to 255, 256 to 511, ...) at most 4 rows name the same one
- live_rows: int32 [512], P(('layer', 'expert')), parts along dimension 0, may hold values from 1 to 256, 24576 in all
- w_down: bfloat16 [512, 384, 1024], P(('layer', 'expert')), parts along dimension 0, may hold values from -0.3125 to 0.3125
- w_moment: bfloat16 [512, 384, 1024], P(('layer', 'expert')), parts along dimension 0, may hold values from -6 to 6
- perm: int32 [512], P('layer'), parts along dimension 0, may hold values from 0 to 127, each once
- fwd_hidden: bfloat16 [131072, 384], P(('layer', 'expert')), parts along dimension 0, may hold values from -6 to 6
- fwd_route: int32 [131072, 1], P(('layer', 'expert')), parts along dimension 0, may hold values from 0 to 127; in each aligned block of 256 rows (0 to 255, 256 to 511, ...) at most 4 rows name the same one
- fwd_gate: float32 [131072], P(('layer', 'expert')), parts along dimension 0, may hold values from 0.25 to 1
Outputs:
- placed_weight: bfloat16 [512, 384, 1024], P(('layer', 'expert')), parts along dimension 0
- placed_moment: bfloat16 [512, 384, 1024], P(('layer', 'expert')), parts along dimension 0
- fwd_out: bfloat16 [131072, 1024], P(('layer', 'expert')), parts along dimension 0
There are 4 independent parts, one for each index of `layer`. A program takes and returns all parts, laid end to end along the dimension named above; each array names one. Nothing has to cross between parts.
Inputs may be any that keep to these rules, and one draw needn't show every extreme that they name: `grad_route`: among the 256 rows of one device no expert is named more than 4 times, and in some device's rows some expert is named exactly 4 times. `fwd_route`: among the 256 rows of one device no expert is named more than 4 times, and in some device's rows some expert is named exactly 4 times. `live_rows`: within each layer the counts sum to three quarters of 32768, and some device has all 256 rows live. `perm`: each device number appears once.
All inputs are finite; a program needn't handle non-finite values.
Results may differ from a plain program's by a relative error of at most 0.0065.
Values may be sent and summed in bfloat16 or wider, within the bound.
A program may use at most 64 MiB of HBM per device.

v0:
```python
import jax
import jax.numpy as jnp
from jax import lax
from jax.sharding import PartitionSpec as P

linear_term = 3.4445
cubic_term = -4.775
quintic_term = 2.0315
moment_decay = 0.9
step_scale = 0.25
norm_floor = 1e-07


def lookup(route_ids, mapping):
    columns = jnp.arange(mapping.shape[0], dtype=jnp.int32)
    hits = route_ids[:, None] == columns[None, :]
    return jnp.sum(jnp.where(hits, mapping[None, :], 0), axis=1)


def slot_matrix(target, is_live, groups, capacity):
    columns = jnp.arange(groups, dtype=jnp.int32)
    onehot = ((target[:, None] == columns[None, :]) & is_live[:, None]).astype(jnp.int32)
    ranked = jnp.sum(jnp.cumsum(onehot, axis=0) * onehot, axis=1) - 1
    slot_of = jnp.where(is_live, target * capacity + ranked, -1)
    slots = jnp.arange(groups * capacity, dtype=jnp.int32)
    return (slots[:, None] == slot_of[None, :]).astype(jnp.bfloat16)


def orthogonalize(moment):
    moment_f = moment.astype(jnp.float32)
    frobenius = jnp.sqrt(jnp.sum(moment_f * moment_f))
    current = (moment_f / (frobenius + norm_floor)).astype(jnp.bfloat16)
    for sweep_index in range(2):
        gramian = lax.dot_general(
            current, current, (((1,), (1,)), ((), ())), preferred_element_type=jnp.float32
        ).astype(jnp.bfloat16)
        squared = jnp.dot(gramian, gramian, preferred_element_type=jnp.float32)
        poly = (cubic_term * gramian.astype(jnp.float32) + quintic_term * squared).astype(
            jnp.bfloat16
        )
        current = (
            linear_term * current.astype(jnp.float32)
            + jnp.dot(poly, current, preferred_element_type=jnp.float32)
        ).astype(jnp.bfloat16)
    return current


def relocate(weight, moment, perm):
    groups = lax.axis_size("expert")
    weight_flat = weight.reshape(groups, -1)
    moment_flat = moment.reshape(groups, -1)
    spread_w, spread_m = (
        lax.all_to_all(weight_flat, "expert", split_axis=0, concat_axis=0, tiled=True),
        lax.all_to_all(moment_flat, "expert", split_axis=0, concat_axis=0, tiled=True),
    )
    devices = jnp.arange(groups, dtype=jnp.int32)
    inverse = jnp.sum(jnp.where(perm[None, :] == devices[:, None], devices[None, :], 0), axis=1)
    ordered_w = jnp.take(spread_w, inverse, axis=0)
    ordered_m = jnp.take(spread_m, inverse, axis=0)
    back_w, back_m = (
        lax.all_to_all(ordered_w, "expert", split_axis=0, concat_axis=0, tiled=True),
        lax.all_to_all(ordered_m, "expert", split_axis=0, concat_axis=0, tiled=True),
    )
    return (back_w.reshape(weight.shape), back_m.reshape(moment.shape))


def per_device(
    grad_hidden,
    grad_out,
    grad_route,
    live_rows,
    w_down,
    w_moment,
    perm,
    fwd_hidden,
    fwd_route,
    fwd_gate,
):
    groups = lax.axis_size("expert")
    grad_count = grad_hidden.shape[0]
    capacity = max(4, 2 * grad_count // groups)
    is_live = jnp.arange(grad_count, dtype=jnp.int32) < live_rows[0]
    route_ids = grad_route[:, 0]
    weight, moment = (w_down, w_moment)
    selector = slot_matrix(route_ids, is_live, groups, capacity)
    hidden_buf = (
        jnp.dot(selector, grad_hidden, preferred_element_type=jnp.float32)
        .astype(jnp.bfloat16)
        .reshape(groups, capacity, -1)
    )
    outgrad_buf = (
        jnp.dot(selector, grad_out, preferred_element_type=jnp.float32)
        .astype(jnp.bfloat16)
        .reshape(groups, capacity, -1)
    )
    recv_hidden, recv_outgrad = (
        lax.all_to_all(hidden_buf, "expert", split_axis=0, concat_axis=0, tiled=True),
        lax.all_to_all(outgrad_buf, "expert", split_axis=0, concat_axis=0, tiled=True),
    )
    grad = lax.dot_general(
        recv_hidden.reshape(groups * capacity, -1),
        recv_outgrad.reshape(groups * capacity, -1),
        (((0,), (0,)), ((), ())),
        preferred_element_type=jnp.float32,
    )
    moment_new = (moment_decay * moment[0].astype(jnp.float32) + grad).astype(jnp.bfloat16)
    ortho = orthogonalize(moment_new)
    weight_new = (weight[0].astype(jnp.float32) - step_scale * ortho.astype(jnp.float32)).astype(
        jnp.bfloat16
    )
    weight_new = weight_new[None]
    moment_new = moment_new[None]
    fwd_ids = fwd_route[:, 0]
    placed_weight, placed_moment = relocate(weight_new, moment_new, perm)
    fwd_target = lookup(fwd_ids, perm)
    fwd_weight = placed_weight[0]
    fwd_count = fwd_hidden.shape[0]
    fwd_capacity = max(4, 2 * fwd_count // groups)
    fwd_selector = slot_matrix(fwd_target, jnp.ones((fwd_count,), dtype=bool), groups, fwd_capacity)
    fwd_buf = (
        jnp.dot(fwd_selector, fwd_hidden, preferred_element_type=jnp.float32)
        .astype(jnp.bfloat16)
        .reshape(groups, fwd_capacity, -1)
    )
    produced = jnp.einsum(
        "gkf,fd->gkd",
        lax.all_to_all(fwd_buf, "expert", split_axis=0, concat_axis=0, tiled=True),
        fwd_weight,
        preferred_element_type=jnp.float32,
    ).astype(jnp.bfloat16)
    returned = lax.all_to_all(produced, "expert", split_axis=0, concat_axis=0, tiled=True)
    fwd_rows_out = lax.dot_general(
        fwd_selector,
        returned.reshape(groups * fwd_capacity, -1),
        (((0,), (0,)), ((), ())),
        preferred_element_type=jnp.float32,
    )
    fwd_out = (fwd_rows_out * fwd_gate[:, None]).astype(jnp.bfloat16)
    return (placed_weight, placed_moment, fwd_out)


def solution(mesh):
    in_specs = (
        P(("layer", "expert"), None),
        P(("layer", "expert"), None),
        P(("layer", "expert"), None),
        P(("layer", "expert")),
        P(("layer", "expert"), None, None),
        P(("layer", "expert"), None, None),
        P("layer"),
        P(("layer", "expert"), None),
        P(("layer", "expert"), None),
        P(("layer", "expert")),
    )
    out_specs = (
        P(("layer", "expert"), None, None),
        P(("layer", "expert"), None, None),
        P(("layer", "expert"), None),
    )
    return jax.shard_map(
        per_device, mesh=mesh, in_specs=in_specs, out_specs=out_specs, check_vma=False
    )
```

profile of v0, /device:TPU:1, one launch (start us, length us, event | category | flops | bytes accessed | tf_op | source)
XLA Modules:
  0.0 438.4 jit_solution(9256716481230762772)
XLA Ops:
  1.4 0.8 copy.49
  2.6 0.9 fusion.27
  3.5 0.7 add_select_fusion
  4.2 1.2 convolution_convert_fusion.3
  5.4 0.8 reshape.115
  6.3 20.6 %all-to-all-start = ((bf16[128,4,384]{2,1,0:T(4,128)(2,1)}), bf16[128,4,384]{2,1,0:T(4,128)(2,1)S(1)}, u32[]{:S(2)}, u32[]{:S(2)}) async-start(bf16[128,4,384]{2,1,0:T(4,128)(2,1)} %reshape.115), calls=%async_computation | async-start | bytes 786432 | tf_op jit(solution)/shard_map/all_to_all | solution.py:97
  27.8 26.9 %all-to-all-done = bf16[128,4,384]{2,1,0:T(4,128)(2,1)S(1)} async-done(((bf16[128,4,384]{2,1,0:T(4,128)(2,1)}), bf16[128,4,384]{2,1,0:T(4,128)(2,1)S(1)}, u32[]{:S(2)}, u32[]{:S(2)}) %all-to-all-start) | async-done | bytes 393248 | tf_op jit(solution)/shard_map/all_to_all | solution.py:97
  54.7 61.6 %all_to_all.64 = bf16[128,4,1024]{2,1,0:T(4,128)(2,1)S(1)} all-to-all(bf16[128,4,1024]{2,1,0:T(4,128)(2,1)S(1)} %reshape.116), channel_id=1, replica_groups=mesh['layer'=4,'expert'=128] {'expert'}, dimensions={0} | all-to-all | bytes 2097152 | tf_op jit(solution)/shard_map/all_to_all | solution.py:98
  116.3 1.6 fusion
  119.2 0.8 add_convert_fusion.1
  121.2 0.9 fusion.2
  123.2 5.3 %reduce.4 = bf16[128,3072]{1,0:T(8,128)(2,1)S(1)} reduce(bf16[128,1,3072]{2,1,0:T(2,128)(2,1)S(1)} %all_to_all.54, bf16[]{:T(256)} %broadcast.131), dimensions={1}, to_apply=%all_to_all.54.reduce_sub_computation | reduce | bytes 1572866 | tf_op jit(solution)/shard_map/all_to_all | solution.py:53
  128.6 1.4 reshape.151
  130.0 9.3 %all-to-all-start.2 = ((bf16[128,2,1536]{2,1,0:T(2,128)(2,1)}), bf16[128,2,1536]{2,1,0:T(2,128)(2,1)}, u32[]{:S(2)}, u32[]{:S(2)}) async-start(bf16[128,2,1536]{2,1,0:T(2,128)(2,1)} %reshape.151), calls=%async_computation.2 | async-start | bytes 1572864 | tf_op jit(solution)/shard_map/all_to_all | solution.py:53
  139.9 5.3 %reduce.3 = bf16[128,3072]{1,0:T(8,128)(2,1)S(1)} reduce(bf16[128,1,3072]{2,1,0:T(2,128)(2,1)S(1)} %all_to_all.55, bf16[]{:T(256)} %broadcast.131), dimensions={1}, to_apply=%all_to_all.55.reduce_sub_computation | reduce | bytes 1572866 | tf_op jit(solution)/shard_map/all_to_all | solution.py:54
  145.3 1.4 reshape.155
  146.7 35.6 %all-to-all-done.2 = bf16[128,2,1536]{2,1,0:T(2,128)(2,1)} async-done(((bf16[128,2,1536]{2,1,0:T(2,128)(2,1)}), bf16[128,2,1536]{2,1,0:T(2,128)(2,1)}, u32[]{:S(2)}, u32[]{:S(2)}) %all-to-all-start.2) | async-done | bytes 786464 | tf_op jit(solution)/shard_map/all_to_all | solution.py:53
  182.3 8.0 %all-to-all-start.4 = ((bf16[128,2,1536]{2,1,0:T(2,128)(2,1)}), bf16[128,2,1536]{2,1,0:T(2,128)(2,1)S(1)}, u32[]{:S(2)}, u32[]{:S(2)}) async-start(bf16[128,2,1536]{2,1,0:T(2,128)(2,1)} %reshape.155), calls=%async_computation.4 | async-start | bytes 1572864 | tf_op jit(solution)/shard_map/all_to_all | solution.py:54
  191.5 0.8 reshape.120
  192.3 41.5 %all-to-all-done.4 = bf16[128,2,1536]{2,1,0:T(2,128)(2,1)S(1)} async-done(((bf16[128,2,1536]{2,1,0:T(2,128)(2,1)}), bf16[128,2,1536]{2,1,0:T(2,128)(2,1)S(1)}, u32[]{:S(2)}, u32[]{:S(2)}) %all-to-all-start.4) | async-done | bytes 786464 | tf_op jit(solution)/shard_map/all_to_all | solution.py:54
  233.8 8.4 %all-to-all-start.6 = ((bf16[128,4,384]{2,1,0:T(4,128)(2,1)}), bf16[128,4,384]{2,1,0:T(4,128)(2,1)S(1)}, u32[]{:S(2)}, u32[]{:S(2)}) async-start(bf16[128,4,384]{2,1,0:T(4,128)(2,1)} %reshape.120), calls=%async_computation.6 | async-start | bytes 786432 | tf_op jit(solution)/shard_map/all_to_all | solution.py:127
  242.4 5.0 %reshape.152 = bf16[128,1,3072]{2,1,0:T(2,128)(2,1)S(1)} reshape(bf16[128,2,1536]{2,1,0:T(2,128)(2,1)} %all-to-all-done.2) | data formatting | bytes 1572864
  247.7 6.0 %reshape.156 = bf16[128,1,3072]{2,1,0:T(2,128)(2,1)} reshape(bf16[128,2,1536]{2,1,0:T(2,128)(2,1)} %copy-done.1) | data formatting | bytes 1572864
  253.7 1.7 copy.75
  255.3 1.0 gather_fusion
  256.4 1.0 gather_fusion.1
  257.4 1.1 select_bitcast_fusion
  258.5 1.1 reduce.5
  259.7 1.4 reshape.153
  261.1 8.8 %all-to-all-done.6 = bf16[128,4,384]{2,1,0:T(4,128)(2,1)S(1)} async-done(((bf16[128,4,384]{2,1,0:T(4,128)(2,1)}), bf16[128,4,384]{2,1,0:T(4,128)(2,1)S(1)}, u32[]{:S(2)}, u32[]{:S(2)}) %all-to-all-start.6) | async-done | bytes 393248 | tf_op jit(solution)/shard_map/all_to_all | solution.py:127
  270.0 7.4 %all-to-all-start.3 = ((bf16[128,2,1536]{2,1,0:T(2,128)(2,1)}), bf16[128,2,1536]{2,1,0:T(2,128)(2,1)S(1)}, u32[]{:S(2)}, u32[]{:S(2)}) async-start(bf16[128,2,1536]{2,1,0:T(2,128)(2,1)} %reshape.153), calls=%async_computation.3 | async-start | bytes 1572864 | tf_op jit(solution)/shard_map/all_to_all | solution.py:61
  277.3 1.1 reduce.6
  278.5 1.5 reshape.157
  279.9 40.9 %all-to-all-done.3 = bf16[128,2,1536]{2,1,0:T(2,128)(2,1)S(1)} async-done(((bf16[128,2,1536]{2,1,0:T(2,128)(2,1)}), bf16[128,2,1536]{2,1,0:T(2,128)(2,1)S(1)}, u32[]{:S(2)}, u32[]{:S(2)}) %all-to-all-start.3) | async-done | bytes 786464 | tf_op jit(solution)/shard_map/all_to_all | solution.py:61
  320.8 0.9 copy-done.2
  321.7 8.9 %all-to-all-start.5 = ((bf16[128,2,1536]{2,1,0:T(2,128)(2,1)}), bf16[128,2,1536]{2,1,0:T(2,128)(2,1)}, u32[]{:S(2)}, u32[]{:S(2)}) async-start(bf16[128,2,1536]{2,1,0:T(2,128)(2,1)} %reshape.157), calls=%async_computation.5 | async-start | bytes 1572864 | tf_op jit(solution)/shard_map/all_to_all | solution.py:62
  330.6 5.0 %reshape.154 = bf16[128,1,3072]{2,1,0:T(2,128)(2,1)S(1)} reshape(bf16[128,2,1536]{2,1,0:T(2,128)(2,1)} %copy-done.2) | data formatting | bytes 1572864
  335.6 4.7 %reduce = bf16[128,3072]{1,0:T(8,128)(2,1)S(1)} reduce(bf16[128,1,3072]{2,1,0:T(2,128)(2,1)S(1)} %reshape.154, bf16[]{:T(256)} %constant.51), dimensions={1}, to_apply=%all_to_all.46.reduce_sub_computation | reduce | bytes 1572866 | tf_op jit(solution)/shard_map/all_to_all | solution.py:61
  340.7 0.7 convolution_convert_fusion
  341.4 1.8 copy.60
  343.3 30.3 %all-to-all-done.5 = bf16[128,2,1536]{2,1,0:T(2,128)(2,1)} async-done(((bf16[128,2,1536]{2,1,0:T(2,128)(2,1)}), bf16[128,2,1536]{2,1,0:T(2,128)(2,1)}, u32[]{:S(2)}, u32[]{:S(2)}) %all-to-all-start.5) | async-done | bytes 786464 | tf_op jit(solution)/shard_map/all_to_all | solution.py:62
  373.6 8.4 %all-to-all-start.7 = ((bf16[128,4,1024]{2,1,0:T(4,128)(2,1)}), bf16[128,4,1024]{2,1,0:T(4,128)(2,1)S(1)}, u32[]{:S(2)}, u32[]{:S(2)}) async-start(bf16[128,4,1024]{2,1,0:T(4,128)(2,1)} %copy.60), calls=%async_computation.7 | async-start | bytes 2097152 | tf_op jit(solution)/shard_map/all_to_all | solution.py:131
  382.1 1.2 reshape.117
  383.3 5.0 %reshape.158 = bf16[128,1,3072]{2,1,0:T(2,128)(2,1)S(1)} reshape(bf16[128,2,1536]{2,1,0:T(2,128)(2,1)} %all-to-all-done.5) | data formatting | bytes 1572864
  388.3 5.6 %reduce.1 = bf16[128,3072]{1,0:T(8,128)(2,1)} reduce(bf16[128,1,3072]{2,1,0:T(2,128)(2,1)S(1)} %reshape.158, bf16[]{:T(256)} %constant.51), dimensions={1}, to_apply=%all_to_all.51.reduce_sub_computation | reduce | bytes 1572866 | tf_op jit(solution)/shard_map/all_to_all | solution.py:62
  394.0 2.2 reshape.118
  396.2 40.2 %all-to-all-done.7 = bf16[128,4,1024]{2,1,0:T(4,128)(2,1)S(1)} async-done(((bf16[128,4,1024]{2,1,0:T(4,128)(2,1)}), bf16[128,4,1024]{2,1,0:T(4,128)(2,1)S(1)}, u32[]{:S(2)}, u32[]{:S(2)}) %all-to-all-start.7) | async-done | bytes 1048608 | tf_op jit(solution)/shard_map/all_to_all | solution.py:131
  436.6 1.3 fusion.4
  (58 shorter events, 7.0 us)
Async XLA Ops:
  0.6 26.2 %copy-start = (bf16[256,1024]{1,0:T(8,128)(2,1)S(1)}, bf16[256,1024]{1,0:T(8,128)(2,1)}, u32[]{:S(2)}) copy-start(bf16[256,1024]{1,0:T(8,128)(2,1)} %param.13) | copy-start | bytes 1572868
  6.3 48.4 %all-to-all-start = ((bf16[128,4,384]{2,1,0:T(4,128)(2,1)}), bf16[128,4,384]{2,1,0:T(4,128)(2,1)S(1)}, u32[]{:S(2)}, u32[]{:S(2)}) async-start(bf16[128,4,384]{2,1,0:T(4,128)(2,1)} %reshape.115), calls=%async_computation | async-start | bytes 786432 | tf_op jit(solution)/shard_map/all_to_all | solution.py:97
  27.7 88.6 %copy-start.9 = (bf16[1,384,1024]{2,1,0:T(8,128)(2,1)S(1)}, bf16[1,384,1024]{2,1,0:T(8,128)(2,1)}, u32[]{:S(2)}) copy-start(bf16[1,384,1024]{2,1,0:T(8,128)(2,1)} %param.17) | copy-start | bytes 2359300
  117.9 1.3 copy-start.4
  120.0 1.1 copy-start.10
  130.0 9.3 %copy-start.5 = (bf16[384,1024]{1,0:T(8,128)(2,1)S(1)}, bf16[384,1024]{1,0:T(8,128)(2,1)}, u32[]{:S(2)}) copy-start(bf16[384,1024]{1,0:T(8,128)(2,1)} %copy-done.4) | copy-start | bytes 2359300
  130.0 52.3 %all-to-all-start.2 = ((bf16[128,2,1536]{2,1,0:T(2,128)(2,1)}), bf16[128,2,1536]{2,1,0:T(2,128)(2,1)}, u32[]{:S(2)}, u32[]{:S(2)}) async-start(bf16[128,2,1536]{2,1,0:T(2,128)(2,1)} %reshape.151), calls=%async_computation.2 | async-start | bytes 1572864 | tf_op jit(solution)/shard_map/all_to_all | solution.py:53
  145.3 45.1 %copy-start.7 = (s32[256,1]{0,1:T(1,128)S(1)}, s32[256,1]{0,1:T(1,128)}, u32[]{:S(2)}) copy-start(s32[256,1]{0,1:T(1,128)} %param.20) | copy-start | bytes 3076
  145.3 45.1 %copy-start.8 = (s32[128]{0:T(128)S(1)}, s32[128]{0:T(128)}, u32[]{:S(2)}) copy-start(s32[128]{0:T(128)} %param.18) | copy-start | bytes 1540
  146.7 44.4 %copy-start.6 = (bf16[256,384]{1,0:T(8,128)(2,1)S(1)}, bf16[256,384]{1,0:T(8,128)(2,1)}, u32[]{:S(2)}) copy-start(bf16[256,384]{1,0:T(8,128)(2,1)} %param.19) | copy-start | bytes 589828
  182.3 51.5 %all-to-all-start.4 = ((bf16[128,2,1536]{2,1,0:T(2,128)(2,1)}), bf16[128,2,1536]{2,1,0:T(2,128)(2,1)S(1)}, u32[]{:S(2)}, u32[]{:S(2)}) async-start(bf16[128,2,1536]{2,1,0:T(2,128)(2,1)} %reshape.155), calls=%async_computation.4 | async-start | bytes 1572864 | tf_op jit(solution)/shard_map/all_to_all | solution.py:54
  233.8 8.6 %copy-start.1 = (bf16[128,2,1536]{2,1,0:T(2,128)(2,1)}, bf16[128,2,1536]{2,1,0:T(2,128)(2,1)S(1)}, u32[]{:S(2)}) copy-start(bf16[128,2,1536]{2,1,0:T(2,128)(2,1)S(1)} %all-to-all-done.4) | copy-start | bytes 2359300
  233.8 36.1 %all-to-all-start.6 = ((bf16[128,4,384]{2,1,0:T(4,128)(2,1)}), bf16[128,4,384]{2,1,0:T(4,128)(2,1)S(1)}, u32[]{:S(2)}, u32[]{:S(2)}) async-start(bf16[128,4,384]{2,1,0:T(4,128)(2,1)} %reshape.120), calls=%async_computation.6 | async-start | bytes 786432 | tf_op jit(solution)/shard_map/all_to_all | solution.py:127
  259.7 17.7 %copy-start.3 = (bf16[128,1,3072]{2,0,1:T(8,128)(2,1)S(1)}, bf16[128,1,3072]{2,0,1:T(8,128)(2,1)}, u32[]{:S(2)}) copy-start(bf16[128,1,3072]{2,0,1:T(8,128)(2,1)} %get-tuple-element.4) | copy-start | bytes 2359300
  270.0 50.8 %all-to-all-start.3 = ((bf16[128,2,1536]{2,1,0:T(2,128)(2,1)}), bf16[128,2,1536]{2,1,0:T(2,128)(2,1)S(1)}, u32[]{:S(2)}, u32[]{:S(2)}) async-start(bf16[128,2,1536]{2,1,0:T(2,128)(2,1)} %reshape.153), calls=%async_computation.3 | async-start | bytes 1572864 | tf_op jit(solution)/shard_map/all_to_all | solution.py:61
  320.8 0.9 copy-start.2
  321.7 51.9 %all-to-all-start.5 = ((bf16[128,2,1536]{2,1,0:T(2,128)(2,1)}), bf16[128,2,1536]{2,1,0:T(2,128)(2,1)}, u32[]{:S(2)}, u32[]{:S(2)}) async-start(bf16[128,2,1536]{2,1,0:T(2,128)(2,1)} %reshape.157), calls=%async_computation.5 | async-start | bytes 1572864 | tf_op jit(solution)/shard_map/all_to_all | solution.py:62
  373.6 62.7 %all-to-all-start.7 = ((bf16[128,4,1024]{2,1,0:T(4,128)(2,1)}), bf16[128,4,1024]{2,1,0:T(4,128)(2,1)S(1)}, u32[]{:S(2)}, u32[]{:S(2)}) async-start(bf16[128,4,1024]{2,1,0:T(4,128)(2,1)} %copy.60), calls=%async_computation.7 | async-start | bytes 2097152 | tf_op jit(solution)/shard_map/all_to_all | solution.py:131
  394.0 42.6 %copy-start.11 = (f32[256]{0:T(256)S(1)}, f32[256]{0:T(256)}, u32[]{:S(2)}) copy-start(f32[256]{0:T(256)} %param.21) | copy-start | bytes 3076
where the time goes:
time: 444 us; the launch traced here: 438 us
  waiting for transfers between devices  224 us (50%)
  starting transfers between devices  71 us (16%)
  blocking collectives  61.6 us (14%)
  local copies, waits for them, and re-layouts  43.1 us (10%)
  other arithmetic  27.1 us (6%)
  matrix products  8.46 us (2%)
    all_to_all x1, blocking collectives, per_device(): lax.all_to_all(outgrad_buf, 'expert', split_axis=0, concat_axis=0, tiled=...  61.6 us
    all_to_all x1, waiting for transfers between devices, relocate(): lax.all_to_all(moment_flat, 'expert', split_axis=0, concat_axis=0, tiled=...  41.5 us
    all_to_all x1, waiting for transfers between devices, relocate(): lax.all_to_all(ordered_w, 'expert', split_axis=0, concat_axis=0, tiled=True)  40.9 us
    all_to_all x1, waiting for transfers between devices, per_device(): lax.all_to_all(produced, 'expert', split_axis=0, concat_axis=0, tiled=True)  40.2 us
    all_to_all x1, waiting for transfers between devices, relocate(): lax.all_to_all(weight_flat, 'expert', split_axis=0, concat_axis=0, tiled=...  35.6 us
    all_to_all x1, waiting for transfers between devices, relocate(): lax.all_to_all(ordered_m, 'expert', split_axis=0, concat_axis=0, tiled=True)  30.3 us
    unnamed x36, local copies, waits for them, and re-layouts  30.3 us
    all_to_all x1, waiting for transfers between devices, per_device(): lax.all_to_all(hidden_buf, 'expert', split_axis=0, concat_axis=0, tiled=T...  26.9 us
  transfers between devices with their start and end apart: 7, of which 7 were waited for; matrix products, arithmetic and copies ran while one was open for 13% of the time, Pallas kernels for 0%

commit v1 on v0

v1 whole, which is shorter than its diff:
```python
import jax
import jax.numpy as jnp
from jax import lax
from jax.experimental import pallas as pl
from jax.experimental.pallas import tpu as pltpu
from jax.sharding import PartitionSpec as P

linear_term = 3.4445
cubic_term = -4.775
quintic_term = 2.0315
moment_decay = 0.9
step_scale = 0.25
norm_floor = 1e-07

Y, Z = 4, 16
CHIPS = Y * Z
EXPERTS = 2 * CHIPS
CAP = 4
ROWS, FF, D = 256, 384, 1024
WIDE = FF + D
PR, PC = 48, 128
PCOLS = D // PC

f32, bf16, i32 = jnp.float32, jnp.bfloat16, jnp.int32


def dot(a, b, dims=(((1,), (0,)), ((), ()))):
    return lax.dot_general(a, b, dims, preferred_element_type=f32)


def piece(ref, p):
    return ref.at[
        pl.ds(pl.multiple_of((p // PCOLS) * PR, 16), PR),
        pl.ds(pl.multiple_of((p % PCOLS) * PC, 128), PC),
    ]


def slots_row(route_row, live):
    experts = lax.broadcasted_iota(i32, (EXPERTS, ROWS), 0)
    hit = experts == route_row
    if live is not None:
        hit = hit & (lax.broadcasted_iota(i32, (EXPERTS, ROWS), 1) < live)
    onehot = jnp.where(hit, 1.0, 0.0)
    r = lax.broadcasted_iota(i32, (ROWS, ROWS), 0)
    q = lax.broadcasted_iota(i32, (ROWS, ROWS), 1)
    before = jnp.where(r < q, 1.0, 0.0).astype(bf16)
    rank = dot(onehot.astype(bf16), before)
    slot = jnp.sum(onehot * (rank + CAP * experts.astype(f32) + 1.0), axis=0, keepdims=True) - 1.0
    return slot.astype(i32)


def slots_col(route_col):
    experts = lax.broadcasted_iota(i32, (ROWS, EXPERTS), 1)
    onehot = jnp.where(experts == route_col, 1.0, 0.0)
    r = lax.broadcasted_iota(i32, (ROWS, ROWS), 0)
    q = lax.broadcasted_iota(i32, (ROWS, ROWS), 1)
    before = jnp.where(q < r, 1.0, 0.0).astype(bf16)
    rank = dot(before, onehot.astype(bf16))
    slot = jnp.sum(onehot * (rank + CAP * experts.astype(f32)), axis=1, keepdims=True)
    return slot.astype(i32)


def kernel(
    live_ref, pos_ref, grow_ref, frow_ref, fcol_ref, gate_ref, hid_ref, og_ref, w_ref, m_ref, fh_ref,
    pw_ref, pm_ref, fo_ref,
    gsend, grecv, gpart, fsend, frecv, rsend, rrecv,
    mnew, wnew, wpart, xm, xw, ym, yw, grad, ortho, gram, poly,
    ssem, rsem, lsem,
):
    idx = lax.axis_index("expert")
    chip, c = idx // 2, idx % 2
    y, z = chip // Z, chip % Z
    partner = {"expert": 2 * chip + 1 - c}

    def peer(u):
        dy, k = u % Y, u // Y
        dz = jnp.where(k % 2 == 1, (k + 1) // 2, Z - k // 2)
        return ((y + dy) % Y) * Z + (z + dz) % Z

    def spread(src_of, dst_ref, n):
        pltpu.make_async_copy(src_of(chip), dst_ref, rsem.at[n]).start()

        @pl.loop(1, CHIPS)
        def _(u):
            t = peer(u)
            pltpu.make_async_remote_copy(
                src_of(t), dst_ref, ssem.at[n], rsem.at[n], device_id={"expert": 2 * t + c}
            ).start()

    def arrived(ref, n):
        pltpu.make_async_copy(ref, ref, rsem.at[n]).wait()

    def to_partner(src_ref, dst_ref, n):
        copy = pltpu.make_async_remote_copy(src_ref, dst_ref, ssem.at[n], rsem.at[n], device_id=partner)
        copy.start()
        return copy

    barrier = pltpu.get_barrier_semaphore()

    @pl.loop(1, CHIPS)
    def _(u):
        pl.semaphore_signal(barrier, inc=1, device_id={"expert": 2 * peer(u) + c})

    pl.semaphore_signal(barrier, inc=1, device_id=partner)

    slot = slots_row(grow_ref[...], live_ref[0])
    slot_ids = lax.broadcasted_iota(i32, (EXPERTS * CAP, ROWS), 0)
    pick = jnp.where(slot_ids == slot, 1.0, 0.0).astype(bf16)
    gsend[:, :, :FF] = dot(pick, hid_ref[...]).reshape(CHIPS, 2 * CAP, FF).astype(bf16)

    @pl.loop(0, D // 256)
    def _(j):
        cols = pl.ds(pl.multiple_of(j * 256, 256), 256)
        out = pl.ds(pl.multiple_of(FF + j * 256, 128), 256)
        gsend[:, :, out] = dot(pick, og_ref[:, cols]).reshape(CHIPS, 2 * CAP, 256).astype(bf16)

    pl.semaphore_wait(barrier, CHIPS)
    spread(lambda t: gsend.at[t], grecv.at[chip], 0)

    fslot = slots_row(frow_ref[...], None)
    fpick = jnp.where(slot_ids == fslot, 1.0, 0.0).astype(bf16)
    fsend[...] = dot(fpick, fh_ref[...]).reshape(CHIPS, 2 * CAP, FF).astype(bf16)
    spread(lambda t: fsend.at[t], frecv.at[chip], 1)

    mine = (lax.broadcasted_iota(i32, (CHIPS, 2 * CAP, 1), 1) // CAP) == c

    def masked_hidden(ref):
        h = ref[:, :, :FF].astype(f32)
        return jnp.where(mine, h, 0.0).reshape(CHIPS * 2 * CAP, FF).astype(bf16)

    def wide_out(ref, cols):
        return ref[:, :, cols].astype(f32).reshape(CHIPS * 2 * CAP, 256).astype(bf16)

    arrived(grecv, 0)
    gcopy = to_partner(grecv, gpart, 2)
    h = masked_hidden(grecv).T

    @pl.loop(0, D // 256)
    def _(j):
        cols = pl.ds(pl.multiple_of(j * 256, 256), 256)
        grad[:, cols] = moment_decay * m_ref[:, cols].astype(f32) + dot(
            h, wide_out(grecv, pl.ds(pl.multiple_of(FF + j * 256, 128), 256))
        )

    gcopy.wait_recv()
    h = masked_hidden(gpart).T

    @pl.loop(0, D // 256)
    def _(j):
        cols = pl.ds(pl.multiple_of(j * 256, 256), 256)
        g = grad[:, cols] + dot(h, wide_out(gpart, pl.ds(pl.multiple_of(FF + j * 256, 128), 256)))
        mnew[:, cols] = g.astype(bf16)

    spread(lambda t: piece(mnew, t), xm.at[c * CHIPS + chip], 3)

    moment = mnew[...].astype(f32)
    frobenius = jnp.sqrt(jnp.sum(moment * moment, keepdims=True))
    ortho[...] = (mnew[...].astype(f32) / (frobenius + norm_floor)).astype(bf16)

    @pl.loop(0, 2)
    def _(_sweep):
        gram[...] = dot(ortho[...], ortho[...], (((1,), (1,)), ((), ()))).astype(bf16)
        squared = dot(gram[...], gram[...])
        poly[...] = (cubic_term * gram[...].astype(f32) + quintic_term * squared).astype(bf16)

        @pl.loop(0, D // 256)
        def _(j):
            cols = pl.ds(pl.multiple_of(j * 256, 256), 256)
            x = ortho[:, cols]
            ortho[:, cols] = (linear_term * x.astype(f32) + dot(poly[...], x)).astype(bf16)

    wnew[...] = (w_ref[...].astype(f32) - step_scale * ortho[...].astype(f32)).astype(bf16)
    wcopy = to_partner(wnew, wpart, 4)
    spread(lambda t: piece(wnew, t), xw.at[c * CHIPS + chip], 5)

    arrived(frecv, 1)
    wcopy.wait_recv()
    x = frecv[...].astype(f32).reshape(CHIPS * 2 * CAP, FF).astype(bf16)

    @pl.loop(0, D // 256)
    def _(j):
        cols = pl.ds(pl.multiple_of(j * 256, 256), 256)
        own = dot(x, wnew[:, cols]).reshape(CHIPS, 2 * CAP, 256)
        other = dot(x, wpart[:, cols]).reshape(CHIPS, 2 * CAP, 256)
        rsend[:, :, cols] = jnp.where(mine, own, other).astype(bf16)

    spread(lambda t: rsend.at[t], rrecv.at[chip], 6)

    def second_hop(x_ref, y_ref, out_ref, first, n):
        own = pl.ds(c * CHIPS, CHIPS)
        arrived(x_ref.at[own], first)
        copy = to_partner(x_ref.at[own], x_ref.at[own], n)
        copy.wait_recv()

        @pl.loop(0, CHIPS)
        def _(t):
            y_ref[t] = x_ref[pos_ref[2 * t + c]]

        spread(lambda t: y_ref.at[t], piece(out_ref, chip), n + 1)
        return copy

    mcopy = second_hop(xm, ym, pm_ref, 3, 7)
    xcopy = second_hop(xw, yw, pw_ref, 5, 9)

    arrived(rrecv, 6)
    fcol = slots_col(fcol_ref[...])
    unpick = jnp.where(lax.broadcasted_iota(i32, (ROWS, EXPERTS * CAP), 1) == fcol, 1.0, 0.0).astype(bf16)

    @pl.loop(0, D // 256)
    def _(j):
        cols = pl.ds(pl.multiple_of(j * 256, 256), 256)
        back = rrecv[:, :, cols].astype(f32).reshape(CHIPS * 2 * CAP, 256).astype(bf16)
        fo_ref[:, cols] = (dot(unpick, back) * gate_ref[...]).astype(bf16)

    arrived(pm_ref, 8)
    arrived(pw_ref, 10)

    for copy in (gcopy, wcopy, mcopy, xcopy):
        copy.wait_send()
    rest = pl.ds(0, CHIPS - 1)
    for ref, n in ((gsend, 0), (fsend, 1), (ym, 3), (yw, 5), (rsend, 6), (ym, 8), (yw, 10)):
        pltpu.make_async_copy(ref.at[rest], ref.at[rest], ssem.at[n]).wait()


def per_device(
    grad_hidden, grad_out, grad_route, live_rows, w_down, w_moment, perm, fwd_hidden, fwd_route, fwd_gate
):
    devices = jnp.arange(EXPERTS, dtype=i32)
    inverse = jnp.sum(jnp.where(perm[None, :] == devices[:, None], devices[None, :], 0), axis=1)
    position = (inverse % 2) * CHIPS + inverse // 2
    smem, vmem = pl.BlockSpec(memory_space=pltpu.SMEM), pl.BlockSpec(memory_space=pltpu.VMEM)
    block = (CHIPS, 2 * CAP)
    pw, pm, fo = pl.pallas_call(
        kernel,
        out_shape=(
            jax.ShapeDtypeStruct((FF, D), bf16),
            jax.ShapeDtypeStruct((FF, D), bf16),
            jax.ShapeDtypeStruct((ROWS, D), bf16),
        ),
        in_specs=[smem, smem] + [vmem] * 9,
        out_specs=(vmem, vmem, vmem),
        scratch_shapes=[
            pltpu.VMEM(block + (WIDE,), bf16),
            pltpu.VMEM(block + (WIDE,), bf16),
            pltpu.VMEM(block + (WIDE,), bf16),
            pltpu.VMEM(block + (FF,), bf16),
            pltpu.VMEM(block + (FF,), bf16),
            pltpu.VMEM(block + (D,), bf16),
            pltpu.VMEM(block + (D,), bf16),
            pltpu.VMEM((FF, D), bf16),
            pltpu.VMEM((FF, D), bf16),
            pltpu.VMEM((FF, D), bf16),
            pltpu.VMEM((EXPERTS, PR, PC), bf16),
            pltpu.VMEM((EXPERTS, PR, PC), bf16),
            pltpu.VMEM((CHIPS, PR, PC), bf16),
            pltpu.VMEM((CHIPS, PR, PC), bf16),
            pltpu.VMEM((FF, D), f32),
            pltpu.VMEM((FF, D), bf16),
            pltpu.VMEM((FF, FF), bf16),
            pltpu.VMEM((FF, FF), bf16),
            pltpu.SemaphoreType.DMA((11,)),
            pltpu.SemaphoreType.DMA((11,)),
            pltpu.SemaphoreType.DMA,
        ],
        compiler_params=pltpu.CompilerParams(collective_id=0, has_side_effects=True),
        name="update_and_move",
    )(
        live_rows, position, grad_route.reshape(1, ROWS), fwd_route.reshape(1, ROWS), fwd_route,
        fwd_gate.reshape(ROWS, 1), grad_hidden, grad_out, w_down[0], w_moment[0], fwd_hidden,
    )
    return pw[None], pm[None], fo


def solution(mesh):
    both = ("layer", "expert")
    in_specs = (
        P(both, None), P(both, None), P(both, None), P(both), P(both, None, None), P(both, None, None),
        P("layer"), P(both, None), P(both, None), P(both),
    )
    out_specs = (P(both, None, None), P(both, None, None), P(both, None))
    return jax.shard_map(per_device, mesh=mesh, in_specs=in_specs, out_specs=out_specs, check_vma=False)
```

time: 444 us -> 296 us (0.67); the launches traced: 438 us -> 295 us
  Pallas kernels: 0 us -> 287 us
  waiting for transfers between devices: 224 us -> 0 us
  starting transfers between devices: 71 us -> 0 us
  blocking collectives: 61.6 us -> 0 us
  local copies, waits for them, and re-layouts: 43.1 us -> 6.67 us
  other arithmetic: 27.1 us -> 0.62 us
  matrix products: 8.46 us -> 0 us
    pallas_call x0 -> x1, Pallas kernels: none -> 287 us  [per_device(): pl.pallas_call(kernel, out_shape=(jax.ShapeDtypeStruct((FF, D), bf16), ja...]
    all_to_all x7 -> x0, waiting for transfers between devices: 224 us -> none  [the longest x1 41.5 us: relocate(): lax.all_to_all(moment_flat, 'expert', split_axis=0, concat_axis=0, tiled=...]
    all_to_all x7 -> x0, starting transfers between devices: 71 us -> none  [the longest x1 20.6 us: per_device(): lax.all_to_all(hidden_buf, 'expert', split_axis=0, concat_axis=0, tiled=T...]
    all_to_all x1 -> x0, blocking collectives: 61.6 us -> none  [per_device(): lax.all_to_all(outgrad_buf, 'expert', split_axis=0, concat_axis=0, tiled=...]
    unnamed x36 -> x14, local copies, waits for them, and re-layouts: 30.3 us -> 5.87 us
    all_to_all x7 -> x0, other arithmetic: 24.3 us -> none  [the longest x3 7.87 us: relocate(): lax.all_to_all(ordered_m, 'expert', split_axis=0, concat_axis=0, tiled=True)]
    dot_general x10 -> x0, matrix products: 8.46 us -> none  [the longest x2 1.7 us: orthogonalize(): jnp.dot(poly, current, preferred_element_type=jnp.float32)]
    reshape x6 -> x1, local copies, waits for them, and re-layouts: 5.8 us -> 0.8 us  [per_device(): fwd_gate.reshape(ROWS, 1)]
  transfers between devices with their start and end apart: 7 -> 0, of which waited for: 7 -> 0; matrix products, arithmetic and copies ran while one was open for 13% -> 0% of each run, Pallas kernels for 0% -> 0%
where the time goes in v1:
time: 296 us; the launch traced here: 295 us
  Pallas kernels  287 us (97%)
  local copies, waits for them, and re-layouts  6.67 us (2%)
    pallas_call x1, Pallas kernels, per_device(): pl.pallas_call(kernel, out_shape=(jax.ShapeDtypeStruct((FF, D), bf16), ja...  287 us

profile of v1, /device:TPU:1, one launch (start us, length us, event | category | flops | bytes accessed | tf_op | source)
XLA Modules:
  0.0 295.4 jit_solution(324776755147012828)
XLA Ops:
  1.3 0.0 copy-start.4
  1.3 0.6 copy-done.4
  1.9 0.1 select_reduce_fusion
  2.0 0.0 copy-start.3
  2.1 0.5 fusion.1.pos_ref
  2.6 0.2 copy-done.3
  2.7 0.0 copy-start.2
  2.7 0.8 copy.17.gate_ref
  3.5 0.0 copy-done.2
  3.5 0.8 copy.16.fcol_ref
  4.3 286.8 %update_and_move.1 = (bf16[384,1024]{1,0:T(8,128)(2,1)}, bf16[384,1024]{1,0:T(8,128)(2,1)}, bf16[256,1024]{1,0:T(8,128)(2,1)}) custom-call(s32[1]{0:T(128)S(6)} %copy.21.live_ref, s32[128]{0:T(128)} %fusion.1.pos_ref, s32[1,256]{1,0:T(1,128)} %bitcast.13, s32[1,256]{1,0:T(1,128)} %bitcast.11, s32[256,1]{1,0:T(8,128)} %copy.16.fcol_ref, ...), custom_call_target="tpu_custom_call" | custom-call | tf_op jit(solution)/shard_map/update_and_move/pallas_call | solution.py:233
  291.1 0.0 copy-start
  291.1 2.1 copy.22
  293.3 0.0 copy-done
  293.3 0.0 copy-start.1
  293.3 0.9 copy.23
  294.1 0.4 copy-done.1
  294.6 0.8 copy.24
Async XLA Ops:
  1.3 0.7 copy-start.4
  2.0 0.7 copy-start.3
  2.7 0.8 copy-start.2
  291.1 2.1 copy-start
  293.3 1.3 copy-start.1

commit v2 on v1

--- a/solution.py
+++ b/solution.py
@@ -33,6 +33,10 @@
         pl.ds(pl.multiple_of((p // PCOLS) * PR, 16), PR),
         pl.ds(pl.multiple_of((p % PCOLS) * PC, 128), PC),
     ]
+
+
+def column(row):
+    return jnp.broadcast_to(row, (128, row.shape[1])).T[:, :1]
 
 
 def slots_row(route_row, live):
@@ -49,20 +53,10 @@
     return slot.astype(i32)
 
 
-def slots_col(route_col):
-    experts = lax.broadcasted_iota(i32, (ROWS, EXPERTS), 1)
-    onehot = jnp.where(experts == route_col, 1.0, 0.0)
-    r = lax.broadcasted_iota(i32, (ROWS, ROWS), 0)
-    q = lax.broadcasted_iota(i32, (ROWS, ROWS), 1)
-    before = jnp.where(q < r, 1.0, 0.0).astype(bf16)
-    rank = dot(before, onehot.astype(bf16))
-    slot = jnp.sum(onehot * (rank + CAP * experts.astype(f32)), axis=1, keepdims=True)
-    return slot.astype(i32)
-
-
 def kernel(
-    live_ref, pos_ref, grow_ref, frow_ref, fcol_ref, gate_ref, hid_ref, og_ref, w_ref, m_ref, fh_ref,
+    live_ref, perm_in, grow_in, frow_in, gate_in, hid_in, og_in, w_in, m_in, fh_in,
     pw_ref, pm_ref, fo_ref,
+    perm_ref, grow_ref, frow_ref, gate_ref, hid_ref, og_ref, w_ref, m_ref, fh_ref, pos_row, pos_ref, unpick, gate_col,
     gsend, grecv, gpart, fsend, frecv, rsend, rrecv,
     mnew, wnew, wpart, xm, xw, ym, yw, grad, ortho, gram, poly,
     ssem, rsem, lsem,
@@ -96,16 +90,31 @@
         return copy
 
     barrier = pltpu.get_barrier_semaphore()
-
-    @pl.loop(1, CHIPS)
-    def _(u):
-        pl.semaphore_signal(barrier, inc=1, device_id={"expert": 2 * peer(u) + c})
-
+    bases = [2 * ((y + dy) % Y) * Z + c for dy in (2, 1, 3, 0)]
+    for dz in sorted(range(Z), key=lambda d: -min(d, Z - d)):
+        z2 = 2 * ((z + dz) % Z)
+        for base in bases[: Y if dz else Y - 1]:
+            pl.semaphore_signal(barrier, inc=1, device_id={"expert": base + z2})
     pl.semaphore_signal(barrier, inc=1, device_id=partner)
 
-    slot = slots_row(grow_ref[...], live_ref[0])
+    loads = [
+        pltpu.make_async_copy(src, dst, lsem.at[n])
+        for n, (src, dst) in enumerate(
+            (
+                (grow_in, grow_ref), (hid_in, hid_ref), (og_in, og_ref), (frow_in, frow_ref), (fh_in, fh_ref),
+                (gate_in, gate_ref), (perm_in, perm_ref), (m_in, m_ref), (w_in, w_ref),
+            )
+        )
+    ]
+    for load in loads:
+        load.start()
+
+    loads[0].wait()
+    slot = slots_row(grow_ref[...], live_ref[...])
     slot_ids = lax.broadcasted_iota(i32, (EXPERTS * CAP, ROWS), 0)
     pick = jnp.where(slot_ids == slot, 1.0, 0.0).astype(bf16)
+    loads[1].wait()
+    loads[2].wait()
     gsend[:, :, :FF] = dot(pick, hid_ref[...]).reshape(CHIPS, 2 * CAP, FF).astype(bf16)
 
     @pl.loop(0, D // 256)
@@ -114,13 +123,28 @@
         out = pl.ds(pl.multiple_of(FF + j * 256, 128), 256)
         gsend[:, :, out] = dot(pick, og_ref[:, cols]).reshape(CHIPS, 2 * CAP, 256).astype(bf16)
 
+    loads[3].wait()
+    fslot = slots_row(frow_ref[...], None)
+    fpick = jnp.where(slot_ids == fslot, 1.0, 0.0).astype(bf16)
+    loads[4].wait()
+    fsend[...] = dot(fpick, fh_ref[...]).reshape(CHIPS, 2 * CAP, FF).astype(bf16)
+
     pl.semaphore_wait(barrier, CHIPS)
     spread(lambda t: gsend.at[t], grecv.at[chip], 0)
-
-    fslot = slots_row(frow_ref[...], None)
-    fpick = jnp.where(slot_ids == fslot, 1.0, 0.0).astype(bf16)
-    fsend[...] = dot(fpick, fh_ref[...]).reshape(CHIPS, 2 * CAP, FF).astype(bf16)
     spread(lambda t: fsend.at[t], frecv.at[chip], 1)
+
+    unpick[...] = fpick.T
+    for load in loads[5:]:
+        load.wait()
+    gate_col[...] = column(gate_ref[...])
+    lanes = lax.broadcasted_iota(i32, (EXPERTS, EXPERTS), 1).astype(f32)
+    source = lax.broadcasted_iota(i32, (EXPERTS, EXPERTS), 0)
+    source = (source % 2) * CHIPS + source // 2
+    moves = lanes == column(perm_ref[...].astype(f32))
+    pos_row[...] = jnp.max(jnp.where(moves, source, 0), axis=0, keepdims=True)
+    pos_copy = pltpu.make_async_copy(pos_row, pos_ref, lsem.at[9])
+    pos_copy.start()
+    pos_copy.wait()
 
     mine = (lax.broadcasted_iota(i32, (CHIPS, 2 * CAP, 1), 1) // CAP) == c
 
@@ -194,7 +218,7 @@
 
         @pl.loop(0, CHIPS)
         def _(t):
-            y_ref[t] = x_ref[pos_ref[2 * t + c]]
+            y_ref[t] = x_ref[pos_ref[0, 2 * t + c]]
 
         spread(lambda t: y_ref.at[t], piece(out_ref, chip), n + 1)
         return copy
@@ -203,14 +227,12 @@
     xcopy = second_hop(xw, yw, pw_ref, 5, 9)
 
     arrived(rrecv, 6)
-    fcol = slots_col(fcol_ref[...])
-    unpick = jnp.where(lax.broadcasted_iota(i32, (ROWS, EXPERTS * CAP), 1) == fcol, 1.0, 0.0).astype(bf16)
 
     @pl.loop(0, D // 256)
     def _(j):
         cols = pl.ds(pl.multiple_of(j * 256, 256), 256)
         back = rrecv[:, :, cols].astype(f32).reshape(CHIPS * 2 * CAP, 256).astype(bf16)
-        fo_ref[:, cols] = (dot(unpick, back) * gate_ref[...]).astype(bf16)
+        fo_ref[:, cols] = (dot(unpick[...], back) * gate_col[...]).astype(bf16)
 
     arrived(pm_ref, 8)
     arrived(pw_ref, 10)
@@ -225,21 +247,31 @@
 def per_device(
     grad_hidden, grad_out, grad_route, live_rows, w_down, w_moment, perm, fwd_hidden, fwd_route, fwd_gate
 ):
-    devices = jnp.arange(EXPERTS, dtype=i32)
-    inverse = jnp.sum(jnp.where(perm[None, :] == devices[:, None], devices[None, :], 0), axis=1)
-    position = (inverse % 2) * CHIPS + inverse // 2
-    smem, vmem = pl.BlockSpec(memory_space=pltpu.SMEM), pl.BlockSpec(memory_space=pltpu.VMEM)
+    vmem, hbm = pl.BlockSpec(memory_space=pltpu.VMEM), pl.BlockSpec(memory_space=pltpu.HBM)
     block = (CHIPS, 2 * CAP)
     pw, pm, fo = pl.pallas_call(
         kernel,
         out_shape=(
-            jax.ShapeDtypeStruct((FF, D), bf16),
-            jax.ShapeDtypeStruct((FF, D), bf16),
-            jax.ShapeDtypeStruct((ROWS, D), bf16),
+            pltpu.VMEM((FF, D), bf16),
+            pltpu.VMEM((FF, D), bf16),
+            pltpu.VMEM((ROWS, D), bf16),
         ),
-        in_specs=[smem, smem] + [vmem] * 9,
+        in_specs=[vmem] + [hbm] * 9,
         out_specs=(vmem, vmem, vmem),
         scratch_shapes=[
+            pltpu.VMEM((1, EXPERTS), i32),
+            pltpu.VMEM((1, ROWS), i32),
+            pltpu.VMEM((1, ROWS), i32),
+            pltpu.VMEM((1, ROWS), f32),
+            pltpu.VMEM((ROWS, FF), bf16),
+            pltpu.VMEM((ROWS, D), bf16),
+            pltpu.VMEM((FF, D), bf16),
+            pltpu.VMEM((FF, D), bf16),
+            pltpu.VMEM((ROWS, FF), bf16),
+            pltpu.VMEM((1, EXPERTS), i32),
+            pltpu.SMEM((1, EXPERTS), i32),
+            pltpu.VMEM((ROWS, EXPERTS * CAP), bf16),
+            pltpu.VMEM((ROWS, 1), f32),
             pltpu.VMEM(block + (WIDE,), bf16),
             pltpu.VMEM(block + (WIDE,), bf16),
             pltpu.VMEM(block + (WIDE,), bf16),
@@ -260,13 +292,14 @@
             pltpu.VMEM((FF, FF), bf16),
             pltpu.SemaphoreType.DMA((11,)),
             pltpu.SemaphoreType.DMA((11,)),
-            pltpu.SemaphoreType.DMA,
+            pltpu.SemaphoreType.DMA((10,)),
         ],
-        compiler_params=pltpu.CompilerParams(collective_id=0, has_side_effects=True),
+        compiler_params=pltpu.CompilerParams(collective_id=0, has_side_effects=True, vmem_limit_bytes=64_930_000),
         name="update_and_move",
     )(
-        live_rows, position, grad_route.reshape(1, ROWS), fwd_route.reshape(1, ROWS), fwd_route,
-        fwd_gate.reshape(ROWS, 1), grad_hidden, grad_out, w_down[0], w_moment[0], fwd_hidden,
+        live_rows.reshape(1, 1), perm.reshape(1, EXPERTS), grad_route.reshape(1, ROWS),
+        fwd_route.reshape(1, ROWS), fwd_gate.reshape(1, ROWS),
+        grad_hidden, grad_out, w_down[0], w_moment[0], fwd_hidden,
     )
     return pw[None], pm[None], fo
 

time: 296 us -> 284 us (0.959)
  Pallas kernels: 287 us -> 277 us
  local copies, waits for them, and re-layouts: 6.67 us -> 2.55 us
    pallas_call x1, Pallas kernels: 287 us -> 277 us  [per_device(): pl.pallas_call(kernel, out_shape=(pltpu.VMEM((FF, D), bf16), pltpu.VMEM((...]
    unnamed x14 -> x3, local copies, waits for them, and re-layouts: 5.87 us -> 2.55 us
where the time goes in v2:
time: 284 us; the launch traced here: 280 us
  Pallas kernels  277 us (98%)
    pallas_call x1, Pallas kernels, per_device(): pl.pallas_call(kernel, out_shape=(pltpu.VMEM((FF, D), bf16), pltpu.VMEM((...  277 us

profile of v2, /device:TPU:1, one launch (start us, length us, event | category | flops | bytes accessed | tf_op | source)
XLA Modules:
  0.0 280.4 jit_solution(8388045752609647364)
XLA Ops:
  1.3 276.6 %update_and_move.1 = (bf16[384,1024]{1,0:T(8,128)(2,1)S(1)}, bf16[384,1024]{1,0:T(8,128)(2,1)S(1)}, bf16[256,1024]{1,0:T(8,128)(2,1)S(1)}) custom-call(s32[1,1]{1,0:T(1,128)} %bitcast.9.live_ref, s32[1,128]{1,0:T(1,128)} %bitcast.17, s32[1,256]{1,0:T(1,128)} %bitcast.14, s32[1,256]{1,0:T(1,128)} %bitcast.15, f32[1,256]{1,0:T(1,128)} %bitcast.16, ...), custom_call_target="tpu_custom_call" | custom-call | tf_op jit(solution)/shard_map/update_and_move/pallas_call | solution.py:252
  277.9 0.9 copy.16
  278.8 0.9 copy.17
  279.6 0.8 copy.18

commit v3 on v2

--- a/solution.py
+++ b/solution.py
@@ -242,6 +242,15 @@
     rest = pl.ds(0, CHIPS - 1)
     for ref, n in ((gsend, 0), (fsend, 1), (ym, 3), (yw, 5), (rsend, 6), (ym, 8), (yw, 10)):
         pltpu.make_async_copy(ref.at[rest], ref.at[rest], ssem.at[n]).wait()
+
+
+def write_out(pw_ref, pm_ref, fo_ref, pw_out, pm_out, fo_out, sem):
+    pairs = ((pw_ref, pw_out), (pm_ref, pm_out), (fo_ref, fo_out))
+    copies = [pltpu.make_async_copy(src, dst, sem.at[n]) for n, (src, dst) in enumerate(pairs)]
+    for copy in copies:
+        copy.start()
+    for copy in copies:
+        copy.wait()
 
 
 def per_device(
@@ -301,6 +310,19 @@
         fwd_route.reshape(1, ROWS), fwd_gate.reshape(1, ROWS),
         grad_hidden, grad_out, w_down[0], w_moment[0], fwd_hidden,
     )
+    pw, pm, fo = pl.pallas_call(
+        write_out,
+        out_shape=(
+            jax.ShapeDtypeStruct((FF, D), bf16),
+            jax.ShapeDtypeStruct((FF, D), bf16),
+            jax.ShapeDtypeStruct((ROWS, D), bf16),
+        ),
+        in_specs=[vmem] * 3,
+        out_specs=(hbm, hbm, hbm),
+        scratch_shapes=[pltpu.SemaphoreType.DMA((3,))],
+        compiler_params=pltpu.CompilerParams(vmem_limit_bytes=1 << 20),
+        name="write_out",
+    )(pw, pm, fo)
     return pw[None], pm[None], fo
 
 

time: 284 us -> 282 us (level)
  no operation moved by 1% of the time
where the time goes in v3:
time: 282 us; the launch traced here: 279 us
  Pallas kernels  278 us (99%)
    pallas_call x1, Pallas kernels, per_device(): pl.pallas_call(kernel, out_shape=(pltpu.VMEM((FF, D), bf16), pltpu.VMEM((...  277 us

profile of v3, /device:TPU:1, one launch (start us, length us, event | category | flops | bytes accessed | tf_op | source)
XLA Modules:
  0.0 279.2 jit_solution(16497703981638843385)
XLA Ops:
  1.3 276.5 %update_and_move.1 = (bf16[384,1024]{1,0:T(8,128)(2,1)S(1)}, bf16[384,1024]{1,0:T(8,128)(2,1)S(1)}, bf16[256,1024]{1,0:T(8,128)(2,1)S(1)}) custom-call(s32[1,1]{1,0:T(1,128)} %bitcast.9.live_ref, s32[1,128]{1,0:T(1,128)} %bitcast.15, s32[1,256]{1,0:T(1,128)} %bitcast.12, s32[1,256]{1,0:T(1,128)} %bitcast.13, f32[1,256]{1,0:T(1,128)} %bitcast.14, ...), custom_call_target="tpu_custom_call" | custom-call | tf_op jit(solution)/shard_map/update_and_move/pallas_call | solution.py:261
  277.8 1.3 write_out.1

commit v4 on v3

--- a/solution.py
+++ b/solution.py
@@ -67,7 +67,7 @@
     partner = {"expert": 2 * chip + 1 - c}
 
     def peer(u):
-        dy, k = u % Y, u // Y
+        dy, k = (CHIPS - u) % Y, (CHIPS - u) // Y
         dz = jnp.where(k % 2 == 1, (k + 1) // 2, Z - k // 2)
         return ((y + dy) % Y) * Z + (z + dz) % Z
 

time: 282 us -> 281 us (level)
  no operation moved by 1% of the time
where the time goes in v4:
time: 281 us
  Pallas kernels  280 us (100%)
    pallas_call x1, Pallas kernels, per_device(): pl.pallas_call(kernel, out_shape=(pltpu.VMEM((FF, D), bf16), pltpu.VMEM((...  278 us

profile of v4, /device:TPU:1, one launch (start us, length us, event | category | flops | bytes accessed | tf_op | source)
XLA Modules:
  0.0 280.9 jit_solution(16328399352128910461)
XLA Ops:
  1.3 278.3 %update_and_move.1 = (bf16[384,1024]{1,0:T(8,128)(2,1)S(1)}, bf16[384,1024]{1,0:T(8,128)(2,1)S(1)}, bf16[256,1024]{1,0:T(8,128)(2,1)S(1)}) custom-call(s32[1,1]{1,0:T(1,128)} %bitcast.9.live_ref, s32[1,128]{1,0:T(1,128)} %bitcast.15, s32[1,256]{1,0:T(1,128)} %bitcast.12, s32[1,256]{1,0:T(1,128)} %bitcast.13, f32[1,256]{1,0:T(1,128)} %bitcast.14, ...), custom_call_target="tpu_custom_call" | custom-call | tf_op jit(solution)/shard_map/update_and_move/pallas_call | solution.py:261
  279.6 1.3 write_out.1
